TPU v7x, 256 devices: a whole 4x4x8 slice. The times are simulated.
256 devices in a mesh: ctx: 64 (over x_hi, y, z), tp: 4 (over x_lo, core).
Axes of the slice: x: 4 (x_hi: 2, x_lo: 2; x = x_hi * 2 + x_lo), y: 4, z: 8, core: 2. Of those that a mesh axis runs over, the one named last changes fastest.
Arguments:
- hidden: bfloat16 [32768, 5120], P('ctx', 'tp'), may hold values from -6 to 6
- queries: bfloat16 [32768, 5120], P('ctx', 'tp'), may hold values from -600 to 600
- lengths: int32 [256], replicated, may hold values from 1 to 2048, 32768 in all
- norm_gain: float32 [5120], P('tp'), may hold values from 0.5 to 1.5
- kv_weight: bfloat16 [5120, 2, 1024], P(None, None, 'tp'), may hold values from -0.078125 to 0.078125
- kv_bias: float32 [2, 1024], P(None, 'tp'), may hold values from -3 to 3
Outputs:
- attended: bfloat16 [32768, 5120], P('ctx', 'tp')
Inputs may be any that keep to these rules, and one draw needn't show every extreme that they name: The 256 files fill the 32768 positions in order; their lengths sum to 32768 and the longest is exactly 2048.
All inputs are finite; a program needn't handle non-finite values.
Results may differ from a plain program's by a relative error of at most 0.006.
Values may be sent and summed in bfloat16 or wider, within the bound.
A program may use at most 128 MiB of HBM per device.

v0:
```python
import jax
import jax.numpy as jnp
from jax import lax
from jax.sharding import PartitionSpec as P

D = 5120
HD = 128
CYCLE = 4


def shifted(value, axis, steps):
    count = lax.axis_size(axis)
    leading, last = (max(0, -steps), min(count, count - steps))
    return lax.ppermute(value, axis, [(source, source + steps) for source in range(leading, last)])


def body(hidden, queries, lengths, norm_gain, kv_weight, kv_bias):
    tok = hidden.shape[0]
    xfull = hidden.astype(jnp.float32)
    squares = lax.psum(jnp.sum(xfull * xfull, axis=1), "tp")
    scale_rows = lax.rsqrt(squares / D + 1e-06)
    normed = (xfull * scale_rows[:, None] * norm_gain[None, :]).astype(jnp.bfloat16)
    flat_weight = kv_weight.reshape(kv_weight.shape[0], -1)
    summed = jnp.dot(
        lax.all_gather(normed, "tp", axis=1, tiled=True),
        flat_weight,
        preferred_element_type=jnp.float32,
    )
    kv_local = (
        (summed + kv_bias.reshape(-1)[None, :])
        .astype(jnp.bfloat16)
        .reshape(tok, 2, kv_weight.shape[2])
    )
    kv_heads = kv_weight.shape[2] // HD
    group = queries.shape[1] // HD // kv_heads
    qrows = queries.reshape(tok, kv_heads, group, HD)
    device = lax.axis_index("ctx")
    ends = jnp.cumsum(lengths)
    score_scale = HD ** (-0.5)

    def docs_of(first):
        positions = first + jnp.arange(tok, dtype=jnp.int32)
        found = jnp.sum((positions[:, None] >= ends[None, :]).astype(jnp.int32), axis=1)
        return (found, positions)

    qdoc, qpos = docs_of(device * tok)

    def attend(state, block, back):
        best, mass, acc = state
        kdoc, kpos = docs_of((device - back) * tok)
        kdoc = jnp.where(device - back >= 0, kdoc, -1)
        keys = block[:, 0].reshape(tok, kv_heads, HD)
        values = block[:, 1].reshape(tok, kv_heads, HD)
        scores = (
            jnp.einsum("qgjd,kgd->gjqk", qrows, keys, preferred_element_type=jnp.float32)
            * score_scale
        )
        visible = (qdoc[:, None] == kdoc[None, :]) & (kpos[None, :] <= qpos[:, None])
        scores = jnp.where(visible[None, None], scores, -1e30)
        top = jnp.maximum(best, jnp.max(scores, axis=-1))
        probs = jnp.exp(scores - top[..., None])
        shrink = jnp.exp(best - top)
        mass = mass * shrink + jnp.sum(probs, axis=-1)
        acc = acc * shrink[..., None] + jnp.einsum(
            "gjqk,kgd->gjqd", probs.astype(jnp.bfloat16), values, preferred_element_type=jnp.float32
        )
        return (top, mass, acc)

    state = (
        jnp.full((kv_heads, group, tok), -1e30, jnp.float32),
        jnp.zeros((kv_heads, group, tok), jnp.float32),
        jnp.zeros((kv_heads, group, tok, HD), jnp.float32),
    )
    state = attend(state, kv_local, 0)
    moving = kv_local
    for back in range(1, CYCLE + 1):
        moving = shifted(moving, "ctx", 1)
        state = attend(state, moving, back)
    best, mass, acc = state
    result = acc / mass[..., None]
    return result.transpose(2, 0, 1, 3).reshape(tok, queries.shape[1]).astype(jnp.bfloat16)


def solution(mesh):
    in_specs = (P("ctx", "tp"), P("ctx", "tp"), P(), P("tp"), P(None, None, "tp"), P(None, "tp"))
    out_specs = P("ctx", "tp")
    return jax.shard_map(body, mesh=mesh, in_specs=in_specs, out_specs=out_specs, check_vma=False)
```

profile of v0, /device:TPU:4, one launch (start us, length us, event | category | flops | bytes accessed | tf_op | source)
XLA Modules:
  0.0 223.8 jit_solution(11458401559064904060)
XLA Ops:
  6.5 1.8 fusion.30
  8.3 6.6 %psum.7 = f32[512]{0:T(512)S(1)} all-reduce(f32[512]{0:T(512)S(1)} %fusion.30), channel_id=1, replica_groups=mesh['ctx'=64,'tp'=4] {'tp'}, use_global_device_ids=true, to_apply=%region_4.5 | all-reduce | flops 512 | bytes 4096 | tf_op jit(solution)/shard_map/psum | solution.py:20
  14.9 2.7 %fusion.32 = bf16[512,1280]{1,0:T(8,128)(2,1)} fusion(bf16[512,1280]{1,0:T(8,128)(2,1)} %param.6, f32[1280]{0:T(1024)} %param.9, f32[512]{0:T(512)S(1)} %add_rsqrt_fusion), kind=kLoop, calls=%fused_computation.39 | loop fusion | flops 2621440 | bytes 2628608 | tf_op jit(solution)/shard_map/convert_element_type | solution.py:22
  17.7 1.0 reduce-window.9
  18.8 5.7 %copy.82 = bf16[640,8,2,256]{3,1,2,0:T(8,128)(2,1)} copy(bf16[640,8,2,256]{3,2,1,0:T(2,128)(2,1)} %bitcast.263) | data formatting | bytes 10485760
  26.4 1.4 compare_and_fusion.4
  27.8 49.7 %all-gather.2.cloned.1.call-done = bf16[512,5120]{1,0:T(8,128)(2,1)} async-done(((bf16[512,1280]{1,0:T(8,128)(2,1)}), bf16[512,5120]{1,0:T(8,128)(2,1)}) %all-gather.2.cloned.1.call-update) | async-done | bytes 5242896 | tf_op jit(solution)/shard_map/all_gather | solution.py:25
  77.5 7.0 %fusion.41 = bf16[512,512]{0,1:T(8,128)(2,1)S(1)} fusion(bf16[512,5120]{1,0:T(8,128)(2,1)} %all-gather.2.cloned.1.call-done, bf16[5120,512]{1,0:T(8,128)(2,1)} %bitcast.264, f32[512]{0:T(512)S(1)} %bitcast.279), kind=kOutput, calls=%fused_computation.52 | convolution fusion | flops 2684878848 | bytes 11012096 | tf_op jit(solution)/shard_map/dot_general | solution.py:24
  84.5 3.5 %collective-permute-start = (bf16[512,2,256]{0,2,1:T(8,128)(2,1)S(1)}, bf16[512,2,256]{0,2,1:T(8,128)(2,1)S(1)}, u32[]{:S(2)}, u32[]{:S(2)}) collective-permute-start(bf16[512,2,256]{0,2,1:T(8,128)(2,1)S(1)} %bitcast.271), channel_id=1, source_target_pairs={{0,4},{4,8},{8,12},{12,16},{16,20},{20,24},{24,28},{28,32},{32,36}... | collective-permute-start | bytes 1572872 | tf_op jit(solution)/shard_map/ppermute | solution.py:14
  88.7 1.9 fusion.10
  90.6 16.3 %collective-permute-done = bf16[512,2,256]{0,2,1:T(8,128)(2,1)S(1)} collective-permute-done((bf16[512,2,256]{0,2,1:T(8,128)(2,1)S(1)}, bf16[512,2,256]{0,2,1:T(8,128)(2,1)S(1)}, u32[]{:S(2)}, u32[]{:S(2)}) %collective-permute-start) | collective-permute-done | bytes 524320 | tf_op jit(solution)/shard_map/ppermute | solution.py:14
  106.9 1.9 collective-permute-start.1
  109.6 5.7 %fusion.11 = (f32[2,5,512]{2,1,0:T(8,128)S(1)}, f32[2,512,512,5]{2,1,3,0:T(8,128)}) fusion(pred[512,512]{0,1:T(8,128)(4,1)S(1)} %get-tuple-element.35, bf16[512,2,128,1]{0,2,3,1:T(8,128)(2,1)S(1)} %bitcast.268, bf16[512,2,5,128]{0,3,2,1:T(8,128)(2,1)S(1)} %bitcast.251), kind=kOutput, calls=%fused_computation.21 | convolution fusion | flops 678947840 | bytes 12341248 | tf_op jit(solution)/shard_map/qgjd,kgd->gjqk/dot_general | solution.py:55
  115.3 13.2 %collective-permute-done.1 = bf16[512,2,256]{0,2,1:T(8,128)(2,1)S(1)} collective-permute-done((bf16[512,2,256]{0,2,1:T(8,128)(2,1)S(1)}, bf16[512,2,256]{0,2,1:T(8,128)(2,1)S(1)}, u32[]{:S(2)}, u32[]{:S(2)}) %collective-permute-start.1) | collective-permute-done | bytes 524320 | tf_op jit(solution)/shard_map/ppermute | solution.py:14
  128.5 2.1 collective-permute-start.2
  131.3 5.9 %fusion.12 = (f32[2,5,512]{2,1,0:T(8,128)S(1)}, f32[2,512,512,5]{2,1,3,0:T(8,128)}) fusion(pred[512,512]{0,1:T(8,128)(4,1)S(1)} %get-tuple-element.32, bf16[512,2,128,1]{0,2,3,1:T(8,128)(2,1)S(1)} %bitcast.269, bf16[512,2,5,128]{0,3,2,1:T(8,128)(2,1)S(1)} %bitcast.252), kind=kOutput, calls=%fused_computation.22 | convolution fusion | flops 678947840 | bytes 12341248 | tf_op jit(solution)/shard_map/qgjd,kgd->gjqk/dot_general | solution.py:55
  137.2 12.0 %collective-permute-done.2 = bf16[512,2,256]{0,2,1:T(8,128)(2,1)S(1)} collective-permute-done((bf16[512,2,256]{0,2,1:T(8,128)(2,1)S(1)}, bf16[512,2,256]{0,2,1:T(8,128)(2,1)S(1)}, u32[]{:S(2)}, u32[]{:S(2)}) %collective-permute-start.2) | collective-permute-done | bytes 524320 | tf_op jit(solution)/shard_map/ppermute | solution.py:14
  149.2 1.9 collective-permute-start.3
  151.8 5.9 %fusion.13 = (f32[2,5,512]{2,1,0:T(8,128)S(1)}, f32[2,512,512,5]{2,1,3,0:T(8,128)}) fusion(pred[512,512]{0,1:T(8,128)(4,1)S(1)} %get-tuple-element.33, bf16[512,2,128,1]{0,2,3,1:T(8,128)(2,1)S(1)} %bitcast.270, bf16[512,2,5,128]{0,3,2,1:T(8,128)(2,1)S(1)} %bitcast.253), kind=kOutput, calls=%fused_computation.23 | convolution fusion | flops 678947840 | bytes 12341248 | tf_op jit(solution)/shard_map/qgjd,kgd->gjqk/dot_general | solution.py:55
  157.7 11.3 %collective-permute-done.3 = bf16[512,2,256]{0,2,1:T(8,128)(2,1)S(1)} collective-permute-done((bf16[512,2,256]{0,2,1:T(8,128)(2,1)S(1)}, bf16[512,2,256]{0,2,1:T(8,128)(2,1)S(1)}, u32[]{:S(2)}, u32[]{:S(2)}) %collective-permute-start.3) | collective-permute-done | bytes 524320 | tf_op jit(solution)/shard_map/ppermute | solution.py:14
  169.7 5.7 %fusion.14 = (f32[2,5,512]{2,1,0:T(8,128)S(1)}, f32[2,512,512,5]{2,1,3,0:T(8,128)}) fusion(pred[512,512]{0,1:T(8,128)(4,1)S(1)} %get-tuple-element.34, bf16[512,2,128,1]{0,2,3,1:T(8,128)(2,1)S(1)} %bitcast.266, bf16[512,2,5,128]{0,3,2,1:T(8,128)(2,1)S(1)} %bitcast.254), kind=kOutput, calls=%fused_computation.24 | convolution fusion | flops 678947840 | bytes 12341248 | tf_op jit(solution)/shard_map/qgjd,kgd->gjqk/dot_general | solution.py:55
  176.1 2.2 fusion
  178.3 5.7 %fusion.23 = f32[2,5,512,128]{2,3,1,0:T(8,128)} fusion(bf16[512,2,128,1]{0,2,3,1:T(8,128)(2,1)} %bitcast.273, f32[2,512,512,5]{2,1,3,0:T(8,128)S(1)} %get-tuple-element.45, f32[2,5,512]{2,1,0:T(8,128)S(1)} %get-tuple-element.30, pred[512,512]{0,1:T(8,128)(4,1)S(1)} %get-tuple-element.31), kind=kOutput, calls=%fused_computation.29 | convolution fusion | flops 681574400 | bytes 13651968 | tf_op jit(solution)/shard_map/gjqk,kgd->gjqd/dot_general | solution.py:64
  184.0 3.0 %fusion.2 = f32[2,5,512]{2,1,0:T(8,128)S(1)} fusion(f32[2,512,512,5]{2,1,3,0:T(8,128)S(1)} %bitcast.256, f32[2,5,512]{2,1,0:T(8,128)} %get-tuple-element.17, pred[512,512]{0,1:T(8,128)(4,1)S(1)} %get-tuple-element.35), kind=kLoop, calls=%fused_computation.12 | loop fusion | flops 10480640 | bytes 10788864 | tf_op jit(solution)/shard_map/reduce_sum | solution.py:63
  187.1 5.0 %fusion.21 = f32[2,5,512,128]{2,3,1,0:T(8,128)} fusion(bf16[512,2,128,1]{0,2,3,1:T(8,128)(2,1)S(1)} %bitcast.275, f32[2,512,512,5]{2,1,3,0:T(8,128)S(1)} %bitcast.256, f32[2,5,512]{2,1,0:T(8,128)} %get-tuple-element.17, pred[512,512]{0,1:T(8,128)(4,1)S(1)} %get-tuple-element.35), kind=kOutput, calls=%fused_computation.28 | convolution fusion | flops 681574400 | bytes 13651968 | tf_op jit(solution)/shard_map/gjqk,kgd->gjqd/dot_general | solution.py:64
  192.1 3.6 %fusion.4 = f32[2,5,512]{2,1,0:T(8,128)} fusion(f32[2,512,512,5]{2,1,3,0:T(8,128)S(1)} %bitcast.260, f32[2,5,512]{2,1,0:T(8,128)} %get-tuple-element.16, pred[512,512]{0,1:T(8,128)(4,1)S(1)} %get-tuple-element.32), kind=kLoop, calls=%fused_computation.14 | loop fusion | flops 10480640 | bytes 10788864 | tf_op jit(solution)/shard_map/reduce_sum | solution.py:63
  195.8 5.0 %fusion.19 = f32[2,5,512,128]{2,3,1,0:T(8,128)} fusion(bf16[512,2,128,1]{0,2,3,1:T(8,128)(2,1)S(1)} %bitcast.276, f32[2,512,512,5]{2,1,3,0:T(8,128)S(1)} %bitcast.260, f32[2,5,512]{2,1,0:T(8,128)} %get-tuple-element.16, pred[512,512]{0,1:T(8,128)(4,1)S(1)} %get-tuple-element.32), kind=kOutput, calls=%fused_computation.27 | convolution fusion | flops 681574400 | bytes 13651968 | tf_op jit(solution)/shard_map/gjqk,kgd->gjqd/dot_general | solution.py:64
  200.8 2.2 fusion.6
  203.0 4.0 %fusion.17 = f32[2,5,512,128]{2,3,1,0:T(8,128)} fusion(bf16[512,2,128,1]{0,2,3,1:T(8,128)(2,1)S(1)} %bitcast.277, f32[2,512,512,5]{2,1,3,0:T(8,128)S(1)} %bitcast.262, f32[2,5,512]{2,1,0:T(8,128)S(1)} %get-tuple-element.15, pred[512,512]{0,1:T(8,128)(4,1)S(1)} %get-tuple-element.33), kind=kOutput, calls=%fused_computation.26 | convolution fusion | flops 681574400 | bytes 13651968 | tf_op jit(solution)/shard_map/gjqk,kgd->gjqd/dot_general | solution.py:64
  207.1 2.2 fusion.8
  210.4 5.1 %fusion.34 = bf16[512,2,5,128]{0,3,2,1:T(8,128)(2,1)S(1)} fusion(f32[2,5,512,128]{2,3,1,0:T(8,128)} %fusion.17, f32[2,5,512,128]{2,3,1,0:T(8,128)S(1)} %copy-done.9, f32[2,5,512,128]{2,3,1,0:T(8,128)S(1)} %copy-done.8, f32[2,5,512,128]{2,3,1,0:T(8,128)S(1)} %copy-done.7, bf16[512,2,128,1]{0,2,3,1:T(8,128)(2,1)S(1)} %bitcast.274, ...), kind=kOutput, calls=%fused_computation.42 | convolution fusion | flops 688783360 | bytes 22949888 | tf_op jit(solution)/shard_map/gjqk,kgd->gjqd/dot_general | solution.py:64
  215.5 1.4 copy.51
  (73 shorter events, 7.4 us)
Async XLA Ops:
  6.5 18.0 %copy-start.6 = (f32[2,256]{1,0:T(2,128)S(1)}, f32[2,256]{1,0:T(2,128)}, u32[]{:S(2)}) copy-start(f32[2,256]{1,0:T(2,128)} %param.11) | copy-start | bytes 6148
  6.5 18.0 %copy-start = (bf16[512,1280]{1,0:T(8,128)(2,1)S(1)}, bf16[512,1280]{1,0:T(8,128)(2,1)}, u32[]{:S(2)}) copy-start(bf16[512,1280]{1,0:T(8,128)(2,1)} %param.7) | copy-start | bytes 3932164
  6.5 71.0 %all-gather.2.cloned.1.call-start = ((), (), s32[]{:S(2)}) async-start(), calls=%async_computation | async-start | bytes 6553600 | tf_op jit(solution)/shard_map/all_gather | solution.py:25
  84.5 22.4 %collective-permute-start = (bf16[512,2,256]{0,2,1:T(8,128)(2,1)S(1)}, bf16[512,2,256]{0,2,1:T(8,128)(2,1)S(1)}, u32[]{:S(2)}, u32[]{:S(2)}) collective-permute-start(bf16[512,2,256]{0,2,1:T(8,128)(2,1)S(1)} %bitcast.271), channel_id=1, source_target_pairs={{0,4},{4,8},{8,12},{12,16},{16,20},{20,24},{24,28},{28,32},{32,36}... | collective-permute-start | bytes 1572872 | tf_op jit(solution)/shard_map/ppermute | solution.py:14
  106.9 21.5 %collective-permute-start.1 = (bf16[512,2,256]{0,2,1:T(8,128)(2,1)S(1)}, bf16[512,2,256]{0,2,1:T(8,128)(2,1)S(1)}, u32[]{:S(2)}, u32[]{:S(2)}) collective-permute-start(bf16[512,2,256]{0,2,1:T(8,128)(2,1)S(1)} %collective-permute-done), channel_id=1, source_target_pairs={{0,4},{4,8},{8,12},{12,16},{16,20},{20,24},{24,28},{28,32},{32,36}... | collective-permute-start | bytes 1572872 | tf_op jit(solution)/shard_map/ppermute | solution.py:14
  128.5 20.7 %collective-permute-start.2 = (bf16[512,2,256]{0,2,1:T(8,128)(2,1)S(1)}, bf16[512,2,256]{0,2,1:T(8,128)(2,1)S(1)}, u32[]{:S(2)}, u32[]{:S(2)}) collective-permute-start(bf16[512,2,256]{0,2,1:T(8,128)(2,1)S(1)} %collective-permute-done.1), channel_id=1, source_target_pairs={{0,4},{4,8},{8,12},{12,16},{16,20},{20,24},{24,28},{28,32},{32,36}... | collective-permute-start | bytes 1572872 | tf_op jit(solution)/shard_map/ppermute | solution.py:14
  149.2 19.8 %collective-permute-start.3 = (bf16[512,2,256]{0,2,1:T(8,128)(2,1)S(1)}, bf16[512,2,256]{0,2,1:T(8,128)(2,1)S(1)}, u32[]{:S(2)}, u32[]{:S(2)}) collective-permute-start(bf16[512,2,256]{0,2,1:T(8,128)(2,1)S(1)} %collective-permute-done.2), channel_id=1, source_target_pairs={{0,4},{4,8},{8,12},{12,16},{16,20},{20,24},{24,28},{28,32},{32,36}... | collective-permute-start | bytes 1572872 | tf_op jit(solution)/shard_map/ppermute | solution.py:14
  176.1 7.9 %slice-start = ((s8[10485760]{0:T(1024)(128)(4,1)}), s8[4194304]{0:T(1024)(128)(4,1)S(1)}, s32[]{:S(2)}) async-start(s8[10485760]{0:T(1024)(128)(4,1)} %bitcast.255), calls=%async_computation.1 | async-start | bytes 8388608
  176.1 7.9 %slice-start.1 = ((s8[10485760]{0:T(1024)(128)(4,1)}), s8[4194304]{0:T(1024)(128)(4,1)S(1)}, s32[]{:S(2)}) async-start(s8[10485760]{0:T(1024)(128)(4,1)} %bitcast.255), calls=%async_computation.2 | async-start | bytes 8388608
  178.3 5.7 %slice-start.2 = ((s8[10485760]{0:T(1024)(128)(4,1)}), s8[2097152]{0:T(1024)(128)(4,1)S(1)}, s32[]{:S(2)}) async-start(s8[10485760]{0:T(1024)(128)(4,1)} %bitcast.255), calls=%async_computation.3 | async-start | bytes 4194304
  183.9 3.1 %copy-start.2 = (bf16[512,1,256]{0,2,1:T(8,128)(2,1)S(1)}, bf16[512,1,256]{0,2,1:T(8,128)(2,1)}, u32[]{:S(2)}) copy-start(bf16[512,1,256]{0,2,1:T(8,128)(2,1)} %get-tuple-element.22) | copy-start | bytes 786436
  184.0 8.1 %slice-start.6 = ((s8[10485760]{0:T(1024)(128)(4,1)}), s8[4194304]{0:T(1024)(128)(4,1)S(1)}, s32[]{:S(2)}) async-start(s8[10485760]{0:T(1024)(128)(4,1)} %bitcast.259), calls=%async_computation.7 | async-start | bytes 8388608
  184.0 8.1 %slice-start.7 = ((s8[10485760]{0:T(1024)(128)(4,1)}), s8[4194304]{0:T(1024)(128)(4,1)S(1)}, s32[]{:S(2)}) async-start(s8[10485760]{0:T(1024)(128)(4,1)} %bitcast.259), calls=%async_computation.8 | async-start | bytes 8388608
  187.1 5.0 %slice-start.8 = ((s8[10485760]{0:T(1024)(128)(4,1)}), s8[2097152]{0:T(1024)(128)(4,1)S(1)}, s32[]{:S(2)}) async-start(s8[10485760]{0:T(1024)(128)(4,1)} %bitcast.259), calls=%async_computation.9 | async-start | bytes 4194304
  192.1 3.7 %copy-start.3 = (bf16[512,1,256]{0,2,1:T(8,128)(2,1)S(1)}, bf16[512,1,256]{0,2,1:T(8,128)(2,1)}, u32[]{:S(2)}) copy-start(bf16[512,1,256]{0,2,1:T(8,128)(2,1)} %get-tuple-element.24) | copy-start | bytes 786436
  192.1 8.7 %slice-start.9 = ((s8[10485760]{0:T(1024)(128)(4,1)}), s8[4194304]{0:T(1024)(128)(4,1)S(1)}, s32[]{:S(2)}) async-start(s8[10485760]{0:T(1024)(128)(4,1)} %bitcast.261), calls=%async_computation.10 | async-start | bytes 8388608
  192.1 8.7 %slice-start.10 = ((s8[10485760]{0:T(1024)(128)(4,1)}), s8[4194304]{0:T(1024)(128)(4,1)S(1)}, s32[]{:S(2)}) async-start(s8[10485760]{0:T(1024)(128)(4,1)} %bitcast.261), calls=%async_computation.11 | async-start | bytes 8388608
  195.8 5.0 %slice-start.11 = ((s8[10485760]{0:T(1024)(128)(4,1)}), s8[2097152]{0:T(1024)(128)(4,1)S(1)}, s32[]{:S(2)}) async-start(s8[10485760]{0:T(1024)(128)(4,1)} %bitcast.261), calls=%async_computation.12 | async-start | bytes 4194304
  195.8 7.2 %copy-start.4 = (bf16[512,1,256]{0,2,1:T(8,128)(2,1)S(1)}, bf16[512,1,256]{0,2,1:T(8,128)(2,1)}, u32[]{:S(2)}) copy-start(bf16[512,1,256]{0,2,1:T(8,128)(2,1)} %get-tuple-element.27) | copy-start | bytes 786436
  200.8 6.3 %slice-start.3 = ((s8[10485760]{0:T(1024)(128)(4,1)}), s8[4194304]{0:T(1024)(128)(4,1)S(1)}, s32[]{:S(2)}) async-start(s8[10485760]{0:T(1024)(128)(4,1)} %bitcast.257), calls=%async_computation.4 | async-start | bytes 8388608
  200.8 6.3 %slice-start.4 = ((s8[10485760]{0:T(1024)(128)(4,1)}), s8[4194304]{0:T(1024)(128)(4,1)S(1)}, s32[]{:S(2)}) async-start(s8[10485760]{0:T(1024)(128)(4,1)} %bitcast.257), calls=%async_computation.5 | async-start | bytes 8388608
  203.0 4.1 %slice-start.5 = ((s8[10485760]{0:T(1024)(128)(4,1)}), s8[2097152]{0:T(1024)(128)(4,1)S(1)}, s32[]{:S(2)}) async-start(s8[10485760]{0:T(1024)(128)(4,1)} %bitcast.257), calls=%async_computation.6 | async-start | bytes 4194304
  203.0 6.3 %copy-start.5 = (f32[2,5,512]{2,1,0:T(8,128)S(1)}, f32[2,5,512]{2,1,0:T(8,128)}, u32[]{:S(2)}) copy-start(f32[2,5,512]{2,1,0:T(8,128)} %fusion.4) | copy-start | bytes 61444
  203.0 6.4 %copy-start.1 = (bf16[512,1,256]{0,2,1:T(8,128)(2,1)S(1)}, bf16[512,1,256]{0,2,1:T(8,128)(2,1)}, u32[]{:S(2)}) copy-start(bf16[512,1,256]{0,2,1:T(8,128)(2,1)} %get-tuple-element.18) | copy-start | bytes 786436
  207.1 2.3 %copy-start.7 = (f32[2,5,512,128]{2,3,1,0:T(8,128)S(1)}, f32[2,5,512,128]{2,3,1,0:T(8,128)}, u32[]{:S(2)}) copy-start(f32[2,5,512,128]{2,3,1,0:T(8,128)} %fusion.23) | copy-start | bytes 7864324
  207.1 2.5 %copy-start.8 = (f32[2,5,512,128]{2,3,1,0:T(8,128)S(1)}, f32[2,5,512,128]{2,3,1,0:T(8,128)}, u32[]{:S(2)}) copy-start(f32[2,5,512,128]{2,3,1,0:T(8,128)} %fusion.21) | copy-start | bytes 7864324
  207.1 3.3 %copy-start.9 = (f32[2,5,512,128]{2,3,1,0:T(8,128)S(1)}, f32[2,5,512,128]{2,3,1,0:T(8,128)}, u32[]{:S(2)}) copy-start(f32[2,5,512,128]{2,3,1,0:T(8,128)} %fusion.19) | copy-start | bytes 7864324
Sparse Core Ops, SparseCore 0:
  17.8 59.6 all-gather.1
where the time goes:
time: 224 us
  waiting for transfers between devices  102 us (46%)
  matrix products  56.9 us (25%)
  other arithmetic  21.9 us (10%)
  between operations  13.8 us (6%)
  local copies, waits for them, and re-layouts  12.8 us (6%)
  starting transfers between devices  9.37 us (4%)
  blocking collectives  6.6 us (3%)
    ppermute x4, waiting for transfers between devices, shifted(): lax.ppermute(value, axis, [(source, source + steps) for source in range(l...  52.7 us
    all_gather x1, waiting for transfers between devices, body(): lax.all_gather(normed, 'tp', axis=1, tiled=True)  49.7 us
    dot_general x5, matrix products, attend(): jnp.einsum('qgjd,kgd->gjqk', qrows, keys, preferred_element_type=jnp.floa...  25.1 us
    dot_general x5, matrix products, attend(): jnp.einsum('gjqk,kgd->gjqd', probs.astype(jnp.bfloat16), values, preferre...  24.8 us
    reduce_sum x5, other arithmetic, attend(): mass = mass * shrink + jnp.sum(probs, axis=-1)  13.2 us
    ppermute x4, starting transfers between devices, shifted(): lax.ppermute(value, axis, [(source, source + steps) for source in range(l...  9.37 us
    unnamed x47, local copies, waits for them, and re-layouts  7.45 us
    dot_general x1, matrix products, body(): jnp.dot(lax.all_gather(normed, 'tp', axis=1, tiled=True), flat_weight, pr...  6.97 us
  transfers between devices with their start and end apart: 5, of which 5 were waited for; matrix products, arithmetic and copies ran while one was open for 14% of the time, Pallas kernels for 0%

commit v1 on v0

--- a/solution.py
+++ b/solution.py
@@ -17,7 +17,7 @@
 def body(hidden, queries, lengths, norm_gain, kv_weight, kv_bias):
     tok = hidden.shape[0]
     xfull = hidden.astype(jnp.float32)
-    squares = lax.psum(jnp.sum(xfull * xfull, axis=1), "tp")
+    squares = jnp.sum(lax.all_gather(jnp.sum(xfull * xfull, axis=1), "tp"), axis=0)
     scale_rows = lax.rsqrt(squares / D + 1e-06)
     normed = (xfull * scale_rows[:, None] * norm_gain[None, :]).astype(jnp.bfloat16)
     flat_weight = kv_weight.reshape(kv_weight.shape[0], -1)

time: 224 us -> 223 us (level)
    psum x1 -> x0, blocking collectives: 6.6 us -> none  [body(): squares = lax.psum(jnp.sum(xfull * xfull, axis=1), 'tp')]
    all_gather x0 -> x1, blocking collectives: none -> 5.16 us  [body(): lax.all_gather(jnp.sum(xfull * xfull, axis=1), 'tp')]
  transfers between devices with their start and end apart: 5 -> 5, of which waited for: 5 -> 5; matrix products, arithmetic and copies ran while one was open for 14% -> 15% of each run, Pallas kernels for 0% -> 0%
where the time goes in v1:
time: 223 us; the launch traced here: 222 us
  waiting for transfers between devices  103 us (46%)
  matrix products  56.9 us (26%)
  other arithmetic  21.9 us (10%)
  between operations  13.8 us (6%)
  local copies, waits for them, and re-layouts  12.8 us (6%)
  starting transfers between devices  9.37 us (4%)
  blocking collectives  5.16 us (2%)
    ppermute x4, waiting for transfers between devices, shifted(): lax.ppermute(value, axis, [(source, source + steps) for source in range(l...  52.7 us
    all_gather x1, waiting for transfers between devices, body(): lax.all_gather(normed, 'tp', axis=1, tiled=True)  49.8 us
    dot_general x5, matrix products, attend(): jnp.einsum('qgjd,kgd->gjqk', qrows, keys, preferred_element_type=jnp.floa...  25.1 us
    dot_general x5, matrix products, attend(): jnp.einsum('gjqk,kgd->gjqd', probs.astype(jnp.bfloat16), values, preferre...  24.8 us
    reduce_sum x5, other arithmetic, attend(): mass = mass * shrink + jnp.sum(probs, axis=-1)  13.2 us
    ppermute x4, starting transfers between devices, shifted(): lax.ppermute(value, axis, [(source, source + steps) for source in range(l...  9.37 us
    unnamed x47, local copies, waits for them, and re-layouts  7.45 us
    dot_general x1, matrix products, body(): jnp.dot(lax.all_gather(normed, 'tp', axis=1, tiled=True), flat_weight, pr...  6.97 us
  transfers between devices with their start and end apart: 5, of which 5 were waited for; matrix products, arithmetic and copies ran while one was open for 15% of the time, Pallas kernels for 0%

profile of v1, /device:TPU:4, one launch (start us, length us, event | category | flops | bytes accessed | tf_op | source)
XLA Modules:
  0.0 222.4 jit_solution(2185084256315874108)
XLA Ops:
  6.5 1.8 fusion.30
  8.3 5.2 %all-gather.1 = f32[4,1,512]{2,1,0:T(1,128)S(1)} all-gather(f32[1,1,512]{2,1,0:T(1,128)S(1)} %bitcast.279), channel_id=2, replica_groups=mesh['ctx'=64,'tp'=4] {'tp'}, dimensions={0}, use_global_device_ids=true | all-gather | bytes 10240 | tf_op jit(solution)/shard_map/all_gather | solution.py:20
  13.5 2.7 %fusion.32 = bf16[512,1280]{1,0:T(8,128)(2,1)} fusion(bf16[512,1280]{1,0:T(8,128)(2,1)} %param.6, f32[1280]{0:T(1024)} %param.9, f32[512]{0:T(512)S(1)} %add_rsqrt_fusion), kind=kLoop, calls=%fused_computation.39 | loop fusion | flops 2621440 | bytes 2628608 | tf_op jit(solution)/shard_map/convert_element_type | solution.py:22
  16.3 1.0 reduce-window.9
  17.4 5.7 %copy.99 = bf16[640,8,2,256]{3,1,2,0:T(8,128)(2,1)} copy(bf16[640,8,2,256]{3,2,1,0:T(2,128)(2,1)} %bitcast.264) | data formatting | bytes 10485760
  25.0 1.4 compare_and_fusion.4
  26.4 49.8 %all-gather.4.cloned.1.call-done = bf16[512,5120]{1,0:T(8,128)(2,1)} async-done(((bf16[512,1280]{1,0:T(8,128)(2,1)}), bf16[512,5120]{1,0:T(8,128)(2,1)}) %all-gather.4.cloned.1.call-update) | async-done | bytes 5242896 | tf_op jit(solution)/shard_map/all_gather | solution.py:25
  76.2 7.0 %fusion.41 = bf16[512,512]{0,1:T(8,128)(2,1)S(1)} fusion(bf16[512,5120]{1,0:T(8,128)(2,1)} %all-gather.4.cloned.1.call-done, bf16[5120,512]{1,0:T(8,128)(2,1)} %bitcast.265, f32[512]{0:T(512)S(1)} %bitcast.281), kind=kOutput, calls=%fused_computation.52 | convolution fusion | flops 2684878848 | bytes 11012096 | tf_op jit(solution)/shard_map/dot_general | solution.py:24
  83.1 3.5 %collective-permute-start = (bf16[512,2,256]{0,2,1:T(8,128)(2,1)S(1)}, bf16[512,2,256]{0,2,1:T(8,128)(2,1)S(1)}, u32[]{:S(2)}, u32[]{:S(2)}) collective-permute-start(bf16[512,2,256]{0,2,1:T(8,128)(2,1)S(1)} %bitcast.272), channel_id=1, source_target_pairs={{0,4},{4,8},{8,12},{12,16},{16,20},{20,24},{24,28},{28,32},{32,36}... | collective-permute-start | bytes 1572872 | tf_op jit(solution)/shard_map/ppermute | solution.py:14
  87.3 1.9 fusion.10
  89.3 16.3 %collective-permute-done = bf16[512,2,256]{0,2,1:T(8,128)(2,1)S(1)} collective-permute-done((bf16[512,2,256]{0,2,1:T(8,128)(2,1)S(1)}, bf16[512,2,256]{0,2,1:T(8,128)(2,1)S(1)}, u32[]{:S(2)}, u32[]{:S(2)}) %collective-permute-start) | collective-permute-done | bytes 524320 | tf_op jit(solution)/shard_map/ppermute | solution.py:14
  105.5 1.9 collective-permute-start.1
  108.2 5.7 %fusion.11 = (f32[2,5,512]{2,1,0:T(8,128)S(1)}, f32[2,512,512,5]{2,1,3,0:T(8,128)}) fusion(pred[512,512]{0,1:T(8,128)(4,1)S(1)} %get-tuple-element.35, bf16[512,2,128,1]{0,2,3,1:T(8,128)(2,1)S(1)} %bitcast.269, bf16[512,2,5,128]{0,3,2,1:T(8,128)(2,1)S(1)} %bitcast.252), kind=kOutput, calls=%fused_computation.21 | convolution fusion | flops 678947840 | bytes 12341248 | tf_op jit(solution)/shard_map/qgjd,kgd->gjqk/dot_general | solution.py:55
  113.9 13.2 %collective-permute-done.1 = bf16[512,2,256]{0,2,1:T(8,128)(2,1)S(1)} collective-permute-done((bf16[512,2,256]{0,2,1:T(8,128)(2,1)S(1)}, bf16[512,2,256]{0,2,1:T(8,128)(2,1)S(1)}, u32[]{:S(2)}, u32[]{:S(2)}) %collective-permute-start.1) | collective-permute-done | bytes 524320 | tf_op jit(solution)/shard_map/ppermute | solution.py:14
  127.1 2.1 collective-permute-start.2
  129.9 5.9 %fusion.12 = (f32[2,5,512]{2,1,0:T(8,128)S(1)}, f32[2,512,512,5]{2,1,3,0:T(8,128)}) fusion(pred[512,512]{0,1:T(8,128)(4,1)S(1)} %get-tuple-element.32, bf16[512,2,128,1]{0,2,3,1:T(8,128)(2,1)S(1)} %bitcast.270, bf16[512,2,5,128]{0,3,2,1:T(8,128)(2,1)S(1)} %bitcast.253), kind=kOutput, calls=%fused_computation.22 | convolution fusion | flops 678947840 | bytes 12341248 | tf_op jit(solution)/shard_map/qgjd,kgd->gjqk/dot_general | solution.py:55
  135.8 12.0 %collective-permute-done.2 = bf16[512,2,256]{0,2,1:T(8,128)(2,1)S(1)} collective-permute-done((bf16[512,2,256]{0,2,1:T(8,128)(2,1)S(1)}, bf16[512,2,256]{0,2,1:T(8,128)(2,1)S(1)}, u32[]{:S(2)}, u32[]{:S(2)}) %collective-permute-start.2) | collective-permute-done | bytes 524320 | tf_op jit(solution)/shard_map/ppermute | solution.py:14
  147.8 1.9 collective-permute-start.3
  150.5 5.9 %fusion.13 = (f32[2,5,512]{2,1,0:T(8,128)S(1)}, f32[2,512,512,5]{2,1,3,0:T(8,128)}) fusion(pred[512,512]{0,1:T(8,128)(4,1)S(1)} %get-tuple-element.33, bf16[512,2,128,1]{0,2,3,1:T(8,128)(2,1)S(1)} %bitcast.271, bf16[512,2,5,128]{0,3,2,1:T(8,128)(2,1)S(1)} %bitcast.254), kind=kOutput, calls=%fused_computation.23 | convolution fusion | flops 678947840 | bytes 12341248 | tf_op jit(solution)/shard_map/qgjd,kgd->gjqk/dot_general | solution.py:55
  156.4 11.3 %collective-permute-done.3 = bf16[512,2,256]{0,2,1:T(8,128)(2,1)S(1)} collective-permute-done((bf16[512,2,256]{0,2,1:T(8,128)(2,1)S(1)}, bf16[512,2,256]{0,2,1:T(8,128)(2,1)S(1)}, u32[]{:S(2)}, u32[]{:S(2)}) %collective-permute-start.3) | collective-permute-done | bytes 524320 | tf_op jit(solution)/shard_map/ppermute | solution.py:14
  168.3 5.7 %fusion.14 = (f32[2,5,512]{2,1,0:T(8,128)S(1)}, f32[2,512,512,5]{2,1,3,0:T(8,128)}) fusion(pred[512,512]{0,1:T(8,128)(4,1)S(1)} %get-tuple-element.34, bf16[512,2,128,1]{0,2,3,1:T(8,128)(2,1)S(1)} %bitcast.267, bf16[512,2,5,128]{0,3,2,1:T(8,128)(2,1)S(1)} %bitcast.255), kind=kOutput, calls=%fused_computation.24 | convolution fusion | flops 678947840 | bytes 12341248 | tf_op jit(solution)/shard_map/qgjd,kgd->gjqk/dot_general | solution.py:55
  174.7 2.2 fusion
  176.9 5.7 %fusion.23 = f32[2,5,512,128]{2,3,1,0:T(8,128)} fusion(bf16[512,2,128,1]{0,2,3,1:T(8,128)(2,1)} %bitcast.274, f32[2,512,512,5]{2,1,3,0:T(8,128)S(1)} %get-tuple-element.45, f32[2,5,512]{2,1,0:T(8,128)S(1)} %get-tuple-element.30, pred[512,512]{0,1:T(8,128)(4,1)S(1)} %get-tuple-element.31), kind=kOutput, calls=%fused_computation.29 | convolution fusion | flops 681574400 | bytes 13651968 | tf_op jit(solution)/shard_map/gjqk,kgd->gjqd/dot_general | solution.py:64
  182.6 3.0 %fusion.2 = f32[2,5,512]{2,1,0:T(8,128)S(1)} fusion(f32[2,512,512,5]{2,1,3,0:T(8,128)S(1)} %bitcast.257, f32[2,5,512]{2,1,0:T(8,128)} %get-tuple-element.17, pred[512,512]{0,1:T(8,128)(4,1)S(1)} %get-tuple-element.35), kind=kLoop, calls=%fused_computation.12 | loop fusion | flops 10480640 | bytes 10788864 | tf_op jit(solution)/shard_map/reduce_sum | solution.py:63
  185.7 5.0 %fusion.21 = f32[2,5,512,128]{2,3,1,0:T(8,128)} fusion(bf16[512,2,128,1]{0,2,3,1:T(8,128)(2,1)S(1)} %bitcast.276, f32[2,512,512,5]{2,1,3,0:T(8,128)S(1)} %bitcast.257, f32[2,5,512]{2,1,0:T(8,128)} %get-tuple-element.17, pred[512,512]{0,1:T(8,128)(4,1)S(1)} %get-tuple-element.35), kind=kOutput, calls=%fused_computation.28 | convolution fusion | flops 681574400 | bytes 13651968 | tf_op jit(solution)/shard_map/gjqk,kgd->gjqd/dot_general | solution.py:64
  190.8 3.6 %fusion.4 = f32[2,5,512]{2,1,0:T(8,128)} fusion(f32[2,512,512,5]{2,1,3,0:T(8,128)S(1)} %bitcast.261, f32[2,5,512]{2,1,0:T(8,128)} %get-tuple-element.16, pred[512,512]{0,1:T(8,128)(4,1)S(1)} %get-tuple-element.32), kind=kLoop, calls=%fused_computation.14 | loop fusion | flops 10480640 | bytes 10788864 | tf_op jit(solution)/shard_map/reduce_sum | solution.py:63
  194.4 5.0 %fusion.19 = f32[2,5,512,128]{2,3,1,0:T(8,128)} fusion(bf16[512,2,128,1]{0,2,3,1:T(8,128)(2,1)S(1)} %bitcast.277, f32[2,512,512,5]{2,1,3,0:T(8,128)S(1)} %bitcast.261, f32[2,5,512]{2,1,0:T(8,128)} %get-tuple-element.16, pred[512,512]{0,1:T(8,128)(4,1)S(1)} %get-tuple-element.32), kind=kOutput, calls=%fused_computation.27 | convolution fusion | flops 681574400 | bytes 13651968 | tf_op jit(solution)/shard_map/gjqk,kgd->gjqd/dot_general | solution.py:64
  199.4 2.2 fusion.6
  201.7 4.0 %fusion.17 = f32[2,5,512,128]{2,3,1,0:T(8,128)} fusion(bf16[512,2,128,1]{0,2,3,1:T(8,128)(2,1)S(1)} %bitcast.278, f32[2,512,512,5]{2,1,3,0:T(8,128)S(1)} %bitcast.263, f32[2,5,512]{2,1,0:T(8,128)S(1)} %get-tuple-element.15, pred[512,512]{0,1:T(8,128)(4,1)S(1)} %get-tuple-element.33), kind=kOutput, calls=%fused_computation.26 | convolution fusion | flops 681574400 | bytes 13651968 | tf_op jit(solution)/shard_map/gjqk,kgd->gjqd/dot_general | solution.py:64
  205.7 2.2 fusion.8
  209.0 5.1 %fusion.34 = bf16[512,2,5,128]{0,3,2,1:T(8,128)(2,1)S(1)} fusion(f32[2,5,512,128]{2,3,1,0:T(8,128)} %fusion.17, f32[2,5,512,128]{2,3,1,0:T(8,128)S(1)} %copy-done.9, f32[2,5,512,128]{2,3,1,0:T(8,128)S(1)} %copy-done.8, f32[2,5,512,128]{2,3,1,0:T(8,128)S(1)} %copy-done.7, bf16[512,2,128,1]{0,2,3,1:T(8,128)(2,1)S(1)} %bitcast.275, ...), kind=kOutput, calls=%fused_computation.42 | convolution fusion | flops 688783360 | bytes 22949888 | tf_op jit(solution)/shard_map/gjqk,kgd->gjqd/dot_general | solution.py:64
  214.1 1.4 copy.68
  (74 shorter events, 7.4 us)
Async XLA Ops:
  6.5 16.6 %copy-start.6 = (f32[2,256]{1,0:T(2,128)S(1)}, f32[2,256]{1,0:T(2,128)}, u32[]{:S(2)}) copy-start(f32[2,256]{1,0:T(2,128)} %param.11) | copy-start | bytes 6148
  6.5 16.6 %copy-start = (bf16[512,1280]{1,0:T(8,128)(2,1)S(1)}, bf16[512,1280]{1,0:T(8,128)(2,1)}, u32[]{:S(2)}) copy-start(bf16[512,1280]{1,0:T(8,128)(2,1)} %param.7) | copy-start | bytes 3932164
  6.5 69.6 %all-gather.4.cloned.1.call-start = ((), (), s32[]{:S(2)}) async-start(), calls=%async_computation | async-start | bytes 6553600 | tf_op jit(solution)/shard_map/all_gather | solution.py:25
  83.1 22.4 %collective-permute-start = (bf16[512,2,256]{0,2,1:T(8,128)(2,1)S(1)}, bf16[512,2,256]{0,2,1:T(8,128)(2,1)S(1)}, u32[]{:S(2)}, u32[]{:S(2)}) collective-permute-start(bf16[512,2,256]{0,2,1:T(8,128)(2,1)S(1)} %bitcast.272), channel_id=1, source_target_pairs={{0,4},{4,8},{8,12},{12,16},{16,20},{20,24},{24,28},{28,32},{32,36}... | collective-permute-start | bytes 1572872 | tf_op jit(solution)/shard_map/ppermute | solution.py:14
  105.5 21.5 %collective-permute-start.1 = (bf16[512,2,256]{0,2,1:T(8,128)(2,1)S(1)}, bf16[512,2,256]{0,2,1:T(8,128)(2,1)S(1)}, u32[]{:S(2)}, u32[]{:S(2)}) collective-permute-start(bf16[512,2,256]{0,2,1:T(8,128)(2,1)S(1)} %collective-permute-done), channel_id=1, source_target_pairs={{0,4},{4,8},{8,12},{12,16},{16,20},{20,24},{24,28},{28,32},{32,36}... | collective-permute-start | bytes 1572872 | tf_op jit(solution)/shard_map/ppermute | solution.py:14
  127.1 20.7 %collective-permute-start.2 = (bf16[512,2,256]{0,2,1:T(8,128)(2,1)S(1)}, bf16[512,2,256]{0,2,1:T(8,128)(2,1)S(1)}, u32[]{:S(2)}, u32[]{:S(2)}) collective-permute-start(bf16[512,2,256]{0,2,1:T(8,128)(2,1)S(1)} %collective-permute-done.1), channel_id=1, source_target_pairs={{0,4},{4,8},{8,12},{12,16},{16,20},{20,24},{24,28},{28,32},{32,36}... | collective-permute-start | bytes 1572872 | tf_op jit(solution)/shard_map/ppermute | solution.py:14
  147.8 19.8 %collective-permute-start.3 = (bf16[512,2,256]{0,2,1:T(8,128)(2,1)S(1)}, bf16[512,2,256]{0,2,1:T(8,128)(2,1)S(1)}, u32[]{:S(2)}, u32[]{:S(2)}) collective-permute-start(bf16[512,2,256]{0,2,1:T(8,128)(2,1)S(1)} %collective-permute-done.2), channel_id=1, source_target_pairs={{0,4},{4,8},{8,12},{12,16},{16,20},{20,24},{24,28},{28,32},{32,36}... | collective-permute-start | bytes 1572872 | tf_op jit(solution)/shard_map/ppermute | solution.py:14
  174.7 7.9 %slice-start = ((s8[10485760]{0:T(1024)(128)(4,1)}), s8[4194304]{0:T(1024)(128)(4,1)S(1)}, s32[]{:S(2)}) async-start(s8[10485760]{0:T(1024)(128)(4,1)} %bitcast.256), calls=%async_computation.1 | async-start | bytes 8388608
  174.7 7.9 %slice-start.1 = ((s8[10485760]{0:T(1024)(128)(4,1)}), s8[4194304]{0:T(1024)(128)(4,1)S(1)}, s32[]{:S(2)}) async-start(s8[10485760]{0:T(1024)(128)(4,1)} %bitcast.256), calls=%async_computation.2 | async-start | bytes 8388608
  176.9 5.7 %slice-start.2 = ((s8[10485760]{0:T(1024)(128)(4,1)}), s8[2097152]{0:T(1024)(128)(4,1)S(1)}, s32[]{:S(2)}) async-start(s8[10485760]{0:T(1024)(128)(4,1)} %bitcast.256), calls=%async_computation.3 | async-start | bytes 4194304
  182.6 3.1 %copy-start.2 = (bf16[512,1,256]{0,2,1:T(8,128)(2,1)S(1)}, bf16[512,1,256]{0,2,1:T(8,128)(2,1)}, u32[]{:S(2)}) copy-start(bf16[512,1,256]{0,2,1:T(8,128)(2,1)} %get-tuple-element.22) | copy-start | bytes 786436
  182.6 8.1 %slice-start.6 = ((s8[10485760]{0:T(1024)(128)(4,1)}), s8[4194304]{0:T(1024)(128)(4,1)S(1)}, s32[]{:S(2)}) async-start(s8[10485760]{0:T(1024)(128)(4,1)} %bitcast.260), calls=%async_computation.7 | async-start | bytes 8388608
  182.6 8.1 %slice-start.7 = ((s8[10485760]{0:T(1024)(128)(4,1)}), s8[4194304]{0:T(1024)(128)(4,1)S(1)}, s32[]{:S(2)}) async-start(s8[10485760]{0:T(1024)(128)(4,1)} %bitcast.260), calls=%async_computation.8 | async-start | bytes 8388608
  185.7 5.0 %slice-start.8 = ((s8[10485760]{0:T(1024)(128)(4,1)}), s8[2097152]{0:T(1024)(128)(4,1)S(1)}, s32[]{:S(2)}) async-start(s8[10485760]{0:T(1024)(128)(4,1)} %bitcast.260), calls=%async_computation.9 | async-start | bytes 4194304
  190.7 3.7 %copy-start.3 = (bf16[512,1,256]{0,2,1:T(8,128)(2,1)S(1)}, bf16[512,1,256]{0,2,1:T(8,128)(2,1)}, u32[]{:S(2)}) copy-start(bf16[512,1,256]{0,2,1:T(8,128)(2,1)} %get-tuple-element.24) | copy-start | bytes 786436
  190.7 8.7 %slice-start.9 = ((s8[10485760]{0:T(1024)(128)(4,1)}), s8[4194304]{0:T(1024)(128)(4,1)S(1)}, s32[]{:S(2)}) async-start(s8[10485760]{0:T(1024)(128)(4,1)} %bitcast.262), calls=%async_computation.10 | async-start | bytes 8388608
  190.7 8.7 %slice-start.10 = ((s8[10485760]{0:T(1024)(128)(4,1)}), s8[4194304]{0:T(1024)(128)(4,1)S(1)}, s32[]{:S(2)}) async-start(s8[10485760]{0:T(1024)(128)(4,1)} %bitcast.262), calls=%async_computation.11 | async-start | bytes 8388608
  194.4 5.0 %slice-start.11 = ((s8[10485760]{0:T(1024)(128)(4,1)}), s8[2097152]{0:T(1024)(128)(4,1)S(1)}, s32[]{:S(2)}) async-start(s8[10485760]{0:T(1024)(128)(4,1)} %bitcast.262), calls=%async_computation.12 | async-start | bytes 4194304
  194.4 7.2 %copy-start.4 = (bf16[512,1,256]{0,2,1:T(8,128)(2,1)S(1)}, bf16[512,1,256]{0,2,1:T(8,128)(2,1)}, u32[]{:S(2)}) copy-start(bf16[512,1,256]{0,2,1:T(8,128)(2,1)} %get-tuple-element.27) | copy-start | bytes 786436
  199.4 6.3 %slice-start.3 = ((s8[10485760]{0:T(1024)(128)(4,1)}), s8[4194304]{0:T(1024)(128)(4,1)S(1)}, s32[]{:S(2)}) async-start(s8[10485760]{0:T(1024)(128)(4,1)} %bitcast.258), calls=%async_computation.4 | async-start | bytes 8388608
  199.4 6.3 %slice-start.4 = ((s8[10485760]{0:T(1024)(128)(4,1)}), s8[4194304]{0:T(1024)(128)(4,1)S(1)}, s32[]{:S(2)}) async-start(s8[10485760]{0:T(1024)(128)(4,1)} %bitcast.258), calls=%async_computation.5 | async-start | bytes 8388608
  201.6 4.1 %slice-start.5 = ((s8[10485760]{0:T(1024)(128)(4,1)}), s8[2097152]{0:T(1024)(128)(4,1)S(1)}, s32[]{:S(2)}) async-start(s8[10485760]{0:T(1024)(128)(4,1)} %bitcast.258), calls=%async_computation.6 | async-start | bytes 4194304
  201.6 6.3 %copy-start.5 = (f32[2,5,512]{2,1,0:T(8,128)S(1)}, f32[2,5,512]{2,1,0:T(8,128)}, u32[]{:S(2)}) copy-start(f32[2,5,512]{2,1,0:T(8,128)} %fusion.4) | copy-start | bytes 61444
  201.6 6.4 %copy-start.1 = (bf16[512,1,256]{0,2,1:T(8,128)(2,1)S(1)}, bf16[512,1,256]{0,2,1:T(8,128)(2,1)}, u32[]{:S(2)}) copy-start(bf16[512,1,256]{0,2,1:T(8,128)(2,1)} %get-tuple-element.18) | copy-start | bytes 786436
  205.7 2.3 %copy-start.7 = (f32[2,5,512,128]{2,3,1,0:T(8,128)S(1)}, f32[2,5,512,128]{2,3,1,0:T(8,128)}, u32[]{:S(2)}) copy-start(f32[2,5,512,128]{2,3,1,0:T(8,128)} %fusion.23) | copy-start | bytes 7864324
  205.7 2.5 %copy-start.8 = (f32[2,5,512,128]{2,3,1,0:T(8,128)S(1)}, f32[2,5,512,128]{2,3,1,0:T(8,128)}, u32[]{:S(2)}) copy-start(f32[2,5,512,128]{2,3,1,0:T(8,128)} %fusion.21) | copy-start | bytes 7864324
  205.7 3.3 %copy-start.9 = (f32[2,5,512,128]{2,3,1,0:T(8,128)S(1)}, f32[2,5,512,128]{2,3,1,0:T(8,128)}, u32[]{:S(2)}) copy-start(f32[2,5,512,128]{2,3,1,0:T(8,128)} %fusion.19) | copy-start | bytes 7864324
Sparse Core Ops, SparseCore 0:
  16.4 59.7 all-gather.3
